TPU v7x, 512 devices: a whole 4x8x8 slice. The times are simulated.
512 devices in a mesh: row: 32 (over z, x_lo, core), col: 16 (over x_hi, y).
Axes of the slice: x: 4 (x_hi: 2, x_lo: 2; x = x_hi * 2 + x_lo), y: 8, z: 8, core: 2. Of those that a mesh axis runs over, the one named last changes fastest.
Arguments:
- slab_block: bfloat16 [65536, 2048], P('row', 'col'), may hold values from -6 to 6
- scale_first: bfloat16 [65536], P('row'), may hold values from 0.5 to 2
- scale_second: bfloat16 [65536], P('row'), may hold values from 0.5 to 2
- panel_lower: bfloat16 [65536, 4096], P('row', 'col'), may hold values from -0.09375 to 0.09375
Outputs:
- updated_slab: bfloat16 [65536, 2048], P('row', 'col')
All inputs are finite; a program needn't handle non-finite values.
Results may differ from a plain program's by a relative error of at most 0.015.
Values may be sent and summed in bfloat16 or wider, within the bound.
No kernel may reach another device: no remote copies, remote signals or barrier semaphores. Data moves between devices by JAX's collectives and lax.ppermute only.
A program may use at most 64 MiB of HBM per device.

v0:
```python
import jax
import jax.numpy as jnp
from jax import lax
from jax.sharding import Mesh, PartitionSpec as P

PANEL_W = 4096
X_HI = 2
CHUNKS = 4
inv_root = 0.7071067811865476


def butterfly(top, bottom):
    top = top.astype(jnp.float32)
    bottom = bottom.astype(jnp.float32)
    return jnp.concatenate([(top + bottom) * inv_root, (top - bottom) * inv_root], axis=0)


def per_device(slab_block, scale_first, scale_second, panel_lower):
    row_count, col_width = slab_block.shape
    groups = lax.axis_size("row")
    y_count = lax.axis_size("y")
    block_width = panel_lower.shape[1]
    chunk = row_count // CHUNKS
    gathered = [
        lax.all_gather(panel_lower[c * chunk : (c + 1) * chunk], "y", axis=1, tiled=True)
        for c in range(CHUNKS)
    ]
    first = (scale_first.astype(jnp.float32)[:, None] * slab_block.astype(jnp.float32)).astype(
        jnp.bfloat16
    )
    cyclic = lax.all_to_all(
        first.reshape(row_count // groups, groups, col_width),
        "row",
        split_axis=1,
        concat_axis=0,
        tiled=True,
    ).reshape(row_count, col_width)
    scale_cyclic = lax.all_to_all(
        scale_second.reshape(row_count // groups, groups),
        "row",
        split_axis=1,
        concat_axis=0,
        tiled=True,
    ).reshape(row_count)
    half = row_count // 2
    quarter = row_count // 4
    level_one = butterfly(cyclic[:half], cyclic[half:])
    second = (scale_cyclic.astype(jnp.float32)[:, None] * level_one).astype(jnp.bfloat16)
    stored = jnp.concatenate(
        [
            butterfly(second[:quarter], second[quarter:half]),
            butterfly(second[half : half + quarter], second[half + quarter :]),
        ],
        axis=0,
    ).astype(jnp.bfloat16)
    top_count = PANEL_W // groups // X_HI
    top = stored[: top_count * X_HI].reshape(1, X_HI, top_count, col_width)
    send = jnp.broadcast_to(top, (groups, X_HI, top_count, col_width)).reshape(
        groups * X_HI, top_count, col_width
    )
    got = lax.all_to_all(send, ("row", "x_hi"), split_axis=0, concat_axis=0)
    got = got.reshape(groups, X_HI, top_count, col_width)
    upper = jnp.transpose(got, (1, 2, 0, 3)).reshape(X_HI, top_count * groups, col_width)
    mine = lax.axis_index("x_hi")
    upper_own = lax.dynamic_index_in_dim(upper, mine, 0, keepdims=False)
    upper_far = lax.dynamic_index_in_dim(upper, 1 - mine, 0, keepdims=False)
    swap = [(i, X_HI - 1 - i) for i in range(X_HI)]
    out = []
    for c in range(CHUNKS):
        far = jnp.dot(gathered[c], upper_far, preferred_element_type=jnp.float32).astype(
            jnp.bfloat16
        )
        came = lax.ppermute(far, "x_hi", swap)
        own = jnp.dot(gathered[c], upper_own, preferred_element_type=jnp.float32)
        base = stored[c * chunk : (c + 1) * chunk].astype(jnp.float32)
        out.append((base - (own + came.astype(jnp.float32))).astype(jnp.bfloat16))
    return jnp.concatenate(out, axis=0)


def solution(mesh):
    rows, cols = mesh.devices.shape
    split = Mesh(mesh.devices.reshape(rows, X_HI, cols // X_HI), ("row", "x_hi", "y"))
    col = ("x_hi", "y")
    placed = (P("row", col), P("row"), P("row"), P("row", col))
    return jax.shard_map(
        per_device, mesh=split, in_specs=placed, out_specs=P("row", col), check_vma=False
    )
```

profile of v0, /device:TPU:16, one launch (start us, length us, event | category | flops | bytes accessed | tf_op | source)
XLA Modules:
  0.0 237.5 jit_solution(13325261711682254845)
XLA Ops:
  6.5 0.0 copy-start.7
  6.5 0.0 all-gather.5.cloned.1.call-start
  6.5 2.3 fusion.47
  8.8 0.0 all-gather.5.cloned.1.call-update
  8.9 0.0 all-gather.7.cloned.1.call-start
  8.9 0.7 all-gather.7.cloned.1.call-update
  9.6 0.0 all-gather.9.cloned.1.call-start
  9.7 0.7 all-gather.9.cloned.1.call-update
  10.3 0.0 copy-done.7
  10.4 0.1 all_to_all.24
  10.4 0.7 copy.21
  11.1 11.6 %all-to-all-start = ((bf16[64,32,1]{0,2,1:T(2,128)(2,1)}), bf16[64,32,1]{0,2,1:T(2,128)(2,1)S(1)}, u32[]{:S(2)}, u32[]{:S(2)}) async-start(bf16[64,32,1]{0,2,1:T(2,128)(2,1)} %copy.21), calls=%async_computation | async-start | bytes 32768 | tf_op jit(solution)/shard_map/all_to_all | solution.py:38
  22.8 0.0 copy-done.8
  22.8 0.0 copy-done.6
  22.8 0.3 multiply_convert_fusion
  23.1 1.0 copy.22
  24.1 6.9 %all-to-all-done = bf16[64,32,1]{0,2,1:T(2,128)(2,1)S(1)} async-done(((bf16[64,32,1]{0,2,1:T(2,128)(2,1)}), bf16[64,32,1]{0,2,1:T(2,128)(2,1)S(1)}, u32[]{:S(2)}, u32[]{:S(2)}) %all-to-all-start) | async-done | bytes 4128 | tf_op jit(solution)/shard_map/all_to_all | solution.py:38
  31.0 3.9 %all-to-all-start.1 = ((bf16[64,32,128]{2,0,1:T(8,128)(2,1)}), bf16[64,32,128]{2,0,1:T(8,128)(2,1)S(1)}, u32[]{:S(2)}, u32[]{:S(2)}) async-start(bf16[64,32,128]{2,0,1:T(8,128)(2,1)} %copy.22), calls=%async_computation.1 | async-start | bytes 1048576 | tf_op jit(solution)/shard_map/all_to_all | solution.py:31
  34.9 0.0 all-gather.11.cloned.1.call-start
  34.9 0.5 all-gather.11.cloned.1.call-update
  35.5 0.1 bitcast_reduce_fusion
  35.5 0.1 reshape.45
  35.6 17.3 %all-to-all-done.1 = bf16[64,32,128]{2,0,1:T(8,128)(2,1)S(1)} async-done(((bf16[64,32,128]{2,0,1:T(8,128)(2,1)}), bf16[64,32,128]{2,0,1:T(8,128)(2,1)S(1)}, u32[]{:S(2)}, u32[]{:S(2)}) %all-to-all-start.1) | async-done | bytes 524320 | tf_op jit(solution)/shard_map/all_to_all | solution.py:31
  52.9 0.1 fusion.5
  53.1 0.2 copy.23
  53.3 0.2 copy.24
  53.5 0.1 fusion.4
  53.5 0.0 copy-start.4
  53.6 0.8 copy-done.4
  54.4 0.1 copy.25
  54.5 1.3 broadcast_in_dim.10
  55.8 5.6 %all-to-all-start.2 = ((bf16[64,64,128]{2,1,0:T(8,128)(2,1)}), bf16[64,64,128]{2,1,0:T(8,128)(2,1)S(1)}, u32[]{:S(2)}, u32[]{:S(2)}) async-start(bf16[64,64,128]{2,1,0:T(8,128)(2,1)} %bitcast.8), calls=%async_computation.2 | async-start | bytes 2097152 | tf_op jit(solution)/shard_map/all_to_all | solution.py:61
  61.5 30.1 %all-to-all-done.2 = bf16[64,64,128]{2,1,0:T(8,128)(2,1)S(1)} async-done(((bf16[64,64,128]{2,1,0:T(8,128)(2,1)}), bf16[64,64,128]{2,1,0:T(8,128)(2,1)S(1)}, u32[]{:S(2)}, u32[]{:S(2)}) %all-to-all-start.2) | async-done | bytes 1048608 | tf_op jit(solution)/shard_map/all_to_all | solution.py:61
  91.6 0.7 copy.26
  92.3 0.0 all-gather.5.cloned.1.call-done
  92.3 3.1 %fusion = bf16[512,128]{0,1:T(8,128)(2,1)} fusion(bf16[512,2048]{1,0:T(8,128)(2,1)} %all-gather.5.cloned.1.call-done, bf16[2,2048,128]{2,1,0:T(8,128)(2,1)S(1)} %bitcast.72, s32[]{:T(128)S(6)} %select_n.8), kind=kOutput, calls=%fused_computation.8 | convolution fusion | flops 268500992 | bytes 2752516 | tf_op jit(solution)/shard_map/dot_general | solution.py:70
  95.4 3.7 %collective-permute-start = (bf16[512,128]{0,1:T(8,128)(2,1)}, bf16[512,128]{0,1:T(8,128)(2,1)S(1)}, u32[]{:S(2)}, u32[]{:S(2)}) collective-permute-start(bf16[512,128]{0,1:T(8,128)(2,1)} %fusion), channel_id=1, source_target_pairs={{0,8},{8,0},{1,9},{9,1},{2,10},{10,2},{3,11},{11,3},{4,12},{12,4},... | collective-permute-start | bytes 393224 | tf_op jit(solution)/shard_map/ppermute | solution.py:73
  99.1 16.7 %all-gather.7.cloned.1.call-done = bf16[512,2048]{1,0:T(8,128)(2,1)} async-done(((bf16[512,256]{1,0:T(8,128)(2,1)}), bf16[512,2048]{1,0:T(8,128)(2,1)}) %all-gather.7.cloned.1.call-update) | async-done | bytes 2097168 | tf_op jit(solution)/shard_map/all_gather | solution.py:25
  115.8 3.1 %fusion.1 = bf16[512,128]{0,1:T(8,128)(2,1)} fusion(bf16[512,2048]{1,0:T(8,128)(2,1)} %all-gather.7.cloned.1.call-done, bf16[2,2048,128]{2,1,0:T(8,128)(2,1)S(1)} %bitcast.73, s32[]{:T(128)S(6)} %select_n.8), kind=kOutput, calls=%fused_computation.9 | convolution fusion | flops 268500992 | bytes 2752516 | tf_op jit(solution)/shard_map/dot_general | solution.py:70
  118.8 3.0 %collective-permute-start.1 = (bf16[512,128]{0,1:T(8,128)(2,1)}, bf16[512,128]{0,1:T(8,128)(2,1)S(1)}, u32[]{:S(2)}, u32[]{:S(2)}) collective-permute-start(bf16[512,128]{0,1:T(8,128)(2,1)} %fusion.1), channel_id=1, source_target_pairs={{0,8},{8,0},{1,9},{9,1},{2,10},{10,2},{3,11},{11,3},{4,12},{12,4},... | collective-permute-start | bytes 393224 | tf_op jit(solution)/shard_map/ppermute | solution.py:73
  121.8 45.2 %all-gather.9.cloned.1.call-done = bf16[512,2048]{1,0:T(8,128)(2,1)} async-done(((bf16[512,256]{1,0:T(8,128)(2,1)}), bf16[512,2048]{1,0:T(8,128)(2,1)}) %all-gather.9.cloned.1.call-update) | async-done | bytes 2097168 | tf_op jit(solution)/shard_map/all_gather | solution.py:25
  167.0 3.1 %fusion.2 = bf16[512,128]{0,1:T(8,128)(2,1)} fusion(bf16[512,2048]{1,0:T(8,128)(2,1)} %all-gather.9.cloned.1.call-done, bf16[2,2048,128]{2,1,0:T(8,128)(2,1)S(1)} %bitcast.74, s32[]{:T(128)S(6)} %select_n.8), kind=kOutput, calls=%fused_computation.10 | convolution fusion | flops 268500992 | bytes 2752516 | tf_op jit(solution)/shard_map/dot_general | solution.py:70
  170.1 2.8 %collective-permute-start.2 = (bf16[512,128]{0,1:T(8,128)(2,1)}, bf16[512,128]{0,1:T(8,128)(2,1)}, u32[]{:S(2)}, u32[]{:S(2)}) collective-permute-start(bf16[512,128]{0,1:T(8,128)(2,1)} %fusion.2), channel_id=1, source_target_pairs={{0,8},{8,0},{1,9},{9,1},{2,10},{10,2},{3,11},{11,3},{4,12},{12,4},... | collective-permute-start | bytes 393224 | tf_op jit(solution)/shard_map/ppermute | solution.py:73
  172.9 45.2 %all-gather.11.cloned.1.call-done = bf16[512,2048]{1,0:T(8,128)(2,1)} async-done(((bf16[512,256]{1,0:T(8,128)(2,1)}), bf16[512,2048]{1,0:T(8,128)(2,1)}) %all-gather.11.cloned.1.call-update) | async-done | bytes 2097168 | tf_op jit(solution)/shard_map/all_gather | solution.py:25
  218.1 2.4 %fusion.3 = bf16[512,128]{0,1:T(8,128)(2,1)S(1)} fusion(bf16[512,2048]{1,0:T(8,128)(2,1)} %all-gather.11.cloned.1.call-done, bf16[2,2048,128]{2,1,0:T(8,128)(2,1)S(1)} %bitcast.75, s32[]{:T(128)S(6)} %select_n.8), kind=kOutput, calls=%fused_computation.11 | convolution fusion | flops 268500992 | bytes 2752516 | tf_op jit(solution)/shard_map/dot_general | solution.py:70
  220.5 0.0 copy-start.1
  220.5 0.0 copy-start.5
  220.5 2.9 %collective-permute-start.3 = (bf16[512,128]{0,1:T(8,128)(2,1)S(1)}, bf16[512,128]{0,1:T(8,128)(2,1)S(1)}, u32[]{:S(2)}, u32[]{:S(2)}) collective-permute-start(bf16[512,128]{0,1:T(8,128)(2,1)S(1)} %fusion.3), channel_id=1, source_target_pairs={{0,8},{8,0},{1,9},{9,1},{2,10},{10,2},{3,11},{11,3},{4,12},{12,4},... | collective-permute-start | bytes 393224 | tf_op jit(solution)/shard_map/ppermute | solution.py:73
  223.5 0.0 collective-permute-done
  223.5 0.0 copy-done
  223.5 0.8 subtract_convert_fusion.3
  224.3 0.0 copy-start.2
  224.3 0.0 collective-permute-done.1
  224.3 0.0 copy-done.1
  224.3 0.0 copy-done.5
  224.4 0.8 subtract_convert_fusion.2
  225.2 0.0 copy-start.3
  225.2 0.0 collective-permute-done.2
  225.2 0.7 copy-done.2
  225.9 1.8 subtract_convert_fusion.1
  227.7 1.4 collective-permute-done.3
  229.0 0.0 copy-done.3
  229.0 0.9 subtract_convert_fusion
  230.0 1.0 copy.27
  (7 shorter events, 0.1 us)
Async XLA Ops:
  6.5 3.8 %copy-start.7 = (bf16[2048]{0:T(1024)(128)(2,1)S(1)}, bf16[2048]{0:T(1024)(128)(2,1)}, u32[]{:S(2)}) copy-start(bf16[2048]{0:T(1024)(128)(2,1)} %param.6) | copy-start | bytes 12292
  6.5 16.2 %copy-start.8 = (bf16[2048]{0:T(1024)(128)(2,1)S(1)}, bf16[2048]{0:T(1024)(128)(2,1)}, u32[]{:S(2)}) copy-start(bf16[2048]{0:T(1024)(128)(2,1)} %param.5) | copy-start | bytes 12292
  6.5 16.3 %copy-start.6 = (bf16[2048,128]{1,0:T(8,128)(2,1)S(1)}, bf16[2048,128]{1,0:T(8,128)(2,1)}, u32[]{:S(2)}) copy-start(bf16[2048,128]{1,0:T(8,128)(2,1)} %param.4) | copy-start | bytes 1572868
  6.5 85.8 %all-gather.5.cloned.1.call-start = ((), (), s32[]{:S(2)}) async-start(), calls=%async_computation.3 | async-start | bytes 2359296 | tf_op jit(solution)/shard_map/all_gather | solution.py:25
  8.9 106.9 %all-gather.7.cloned.1.call-start = ((), (), s32[]{:S(2)}) async-start(), calls=%async_computation.4 | async-start | bytes 2359296 | tf_op jit(solution)/shard_map/all_gather | solution.py:25
  9.6 157.4 %all-gather.9.cloned.1.call-start = ((), (), s32[]{:S(2)}) async-start(), calls=%async_computation.5 | async-start | bytes 2359296 | tf_op jit(solution)/shard_map/all_gather | solution.py:25
  11.1 19.9 %all-to-all-start = ((bf16[64,32,1]{0,2,1:T(2,128)(2,1)}), bf16[64,32,1]{0,2,1:T(2,128)(2,1)S(1)}, u32[]{:S(2)}, u32[]{:S(2)}) async-start(bf16[64,32,1]{0,2,1:T(2,128)(2,1)} %copy.21), calls=%async_computation | async-start | bytes 32768 | tf_op jit(solution)/shard_map/all_to_all | solution.py:38
  31.0 21.9 %all-to-all-start.1 = ((bf16[64,32,128]{2,0,1:T(8,128)(2,1)}), bf16[64,32,128]{2,0,1:T(8,128)(2,1)S(1)}, u32[]{:S(2)}, u32[]{:S(2)}) async-start(bf16[64,32,128]{2,0,1:T(8,128)(2,1)} %copy.22), calls=%async_computation.1 | async-start | bytes 1048576 | tf_op jit(solution)/shard_map/all_to_all | solution.py:31
  34.9 183.2 %all-gather.11.cloned.1.call-start = ((), (), s32[]{:S(2)}) async-start(), calls=%async_computation.6 | async-start | bytes 2359296 | tf_op jit(solution)/shard_map/all_gather | solution.py:25
  53.5 0.8 copy-start.4
  55.8 35.8 %all-to-all-start.2 = ((bf16[64,64,128]{2,1,0:T(8,128)(2,1)}), bf16[64,64,128]{2,1,0:T(8,128)(2,1)S(1)}, u32[]{:S(2)}, u32[]{:S(2)}) async-start(bf16[64,64,128]{2,1,0:T(8,128)(2,1)} %bitcast.8), calls=%async_computation.2 | async-start | bytes 2097152 | tf_op jit(solution)/shard_map/all_to_all | solution.py:61
  95.4 128.1 %collective-permute-start = (bf16[512,128]{0,1:T(8,128)(2,1)}, bf16[512,128]{0,1:T(8,128)(2,1)S(1)}, u32[]{:S(2)}, u32[]{:S(2)}) collective-permute-start(bf16[512,128]{0,1:T(8,128)(2,1)} %fusion), channel_id=1, source_target_pairs={{0,8},{8,0},{1,9},{9,1},{2,10},{10,2},{3,11},{11,3},{4,12},{12,4},... | collective-permute-start | bytes 393224 | tf_op jit(solution)/shard_map/ppermute | solution.py:73
  118.8 104.6 %copy-start = (bf16[512,2048]{1,0:T(8,128)(2,1)S(1)}, bf16[512,2048]{1,0:T(8,128)(2,1)}, u32[]{:S(2)}) copy-start(bf16[512,2048]{1,0:T(8,128)(2,1)} %all-gather.5.cloned.1.call-done) | copy-start | bytes 6291460
  118.8 105.5 %collective-permute-start.1 = (bf16[512,128]{0,1:T(8,128)(2,1)}, bf16[512,128]{0,1:T(8,128)(2,1)S(1)}, u32[]{:S(2)}, u32[]{:S(2)}) collective-permute-start(bf16[512,128]{0,1:T(8,128)(2,1)} %fusion.1), channel_id=1, source_target_pairs={{0,8},{8,0},{1,9},{9,1},{2,10},{10,2},{3,11},{11,3},{4,12},{12,4},... | collective-permute-start | bytes 393224 | tf_op jit(solution)/shard_map/ppermute | solution.py:73
  170.1 55.1 %collective-permute-start.2 = (bf16[512,128]{0,1:T(8,128)(2,1)}, bf16[512,128]{0,1:T(8,128)(2,1)}, u32[]{:S(2)}, u32[]{:S(2)}) collective-permute-start(bf16[512,128]{0,1:T(8,128)(2,1)} %fusion.2), channel_id=1, source_target_pairs={{0,8},{8,0},{1,9},{9,1},{2,10},{10,2},{3,11},{11,3},{4,12},{12,4},... | collective-permute-start | bytes 393224 | tf_op jit(solution)/shard_map/ppermute | solution.py:73
  220.5 3.8 %copy-start.1 = (bf16[512,2048]{1,0:T(8,128)(2,1)S(1)}, bf16[512,2048]{1,0:T(8,128)(2,1)}, u32[]{:S(2)}) copy-start(bf16[512,2048]{1,0:T(8,128)(2,1)} %all-gather.7.cloned.1.call-done) | copy-start | bytes 6291460
  220.5 3.8 %copy-start.5 = (bf16[2048,128]{0,1:T(8,128)(2,1)S(1)}, bf16[2048,128]{0,1:T(8,128)(2,1)}, u32[]{:S(2)}) copy-start(bf16[2048,128]{0,1:T(8,128)(2,1)} %copy-done.4) | copy-start | bytes 1572868
  220.5 8.5 %collective-permute-start.3 = (bf16[512,128]{0,1:T(8,128)(2,1)S(1)}, bf16[512,128]{0,1:T(8,128)(2,1)S(1)}, u32[]{:S(2)}, u32[]{:S(2)}) collective-permute-start(bf16[512,128]{0,1:T(8,128)(2,1)S(1)} %fusion.3), channel_id=1, source_target_pairs={{0,8},{8,0},{1,9},{9,1},{2,10},{10,2},{3,11},{11,3},{4,12},{12,4},... | collective-permute-start | bytes 393224 | tf_op jit(solution)/shard_map/ppermute | solution.py:73
  224.3 1.6 copy-start.2
  225.2 3.8 %copy-start.3 = (bf16[512,2048]{1,0:T(8,128)(2,1)S(1)}, bf16[512,2048]{1,0:T(8,128)(2,1)}, u32[]{:S(2)}) copy-start(bf16[512,2048]{1,0:T(8,128)(2,1)} %all-gather.11.cloned.1.call-done) | copy-start | bytes 6291460
Sparse Core Ops, SparseCore 0:
  9.4 55.1 all-gather.4
  66.6 49.1 all-gather.6
  117.8 49.2 all-gather.8
  168.9 49.1 all-gather.10
where the time goes:
time: 238 us; the launch traced here: 237 us
  waiting for transfers between devices  165 us (69%)
  starting transfers between devices  33.6 us (14%)
  matrix products  15.9 us (7%)
  between operations  13.4 us (6%)
  local copies, waits for them, and re-layouts  9.13 us (4%)
    all_gather x4, waiting for transfers between devices, per_device(): lax.all_gather(panel_lower[c * chunk:(c + 1) * chunk], 'y', axis=1, tiled...  107 us
    all_to_all x1, waiting for transfers between devices, per_device(): got = lax.all_to_all(send, ('row', 'x_hi'), split_axis=0, concat_axis=0)  30.1 us
    all_to_all x1, waiting for transfers between devices, per_device(): lax.all_to_all(first.reshape(row_count // groups, groups, col_width), 'ro...  17.3 us
    ppermute x4, starting transfers between devices, per_device(): came = lax.ppermute(far, 'x_hi', swap)  12.3 us
    dot_general x4, matrix products, per_device(): jnp.dot(gathered[c], upper_far, preferred_element_type=jnp.float32)  11.7 us
    all_to_all x1, starting transfers between devices, per_device(): lax.all_to_all(scale_second.reshape(row_count // groups, groups), 'row',...  11.6 us
    all_to_all x1, waiting for transfers between devices, per_device(): lax.all_to_all(scale_second.reshape(row_count // groups, groups), 'row',...  6.85 us
    all_to_all x1, starting transfers between devices, per_device(): got = lax.all_to_all(send, ('row', 'x_hi'), split_axis=0, concat_axis=0)  5.65 us
  transfers between devices with their start and end apart: 11, of which 7 were waited for; matrix products, arithmetic and copies ran while one was open for 8% of the time, Pallas kernels for 0%

commit v1 on v0

--- a/solution.py
+++ b/solution.py
@@ -21,10 +21,12 @@
     y_count = lax.axis_size("y")
     block_width = panel_lower.shape[1]
     chunk = row_count // CHUNKS
-    gathered = [
-        lax.all_gather(panel_lower[c * chunk : (c + 1) * chunk], "y", axis=1, tiled=True)
-        for c in range(CHUNKS)
-    ]
+
+    def wrap_surface_on(unit):
+        view_out = lax.all_to_all(jnp.stack([unit] * lax.axis_size("y")), "y", 0, 0)
+        return jnp.concatenate(view_out, axis=1)
+
+    gathered = [wrap_surface_on(panel_lower[c * chunk : (c + 1) * chunk]) for c in range(CHUNKS)]
     first = (scale_first.astype(jnp.float32)[:, None] * slab_block.astype(jnp.float32)).astype(
         jnp.bfloat16
     )

time: 238 us -> 323 us (1.36)
  the two profiles are of different devices: /device:TPU:16 before, /device:TPU:10 now
where the time goes in v1:
time: 323 us; the launch traced here: 322 us
  waiting for transfers between devices  227 us (70%)
  starting transfers between devices  60.5 us (19%)
  local copies, waits for them, and re-layouts  16.6 us (5%)
  matrix products  14.8 us (5%)
    all_to_all x4, waiting for transfers between devices, wrap_surface_on(): view_out = lax.all_to_all(jnp.stack([unit] * lax.axis_size('y')), 'y', 0, 0)  178 us
    all_to_all x1, waiting for transfers between devices, per_device(): got = lax.all_to_all(send, ('row', 'x_hi'), split_axis=0, concat_axis=0)  27.8 us
    all_to_all x4, starting transfers between devices, wrap_surface_on(): view_out = lax.all_to_all(jnp.stack([unit] * lax.axis_size('y')), 'y', 0, 0)  23.5 us
    all_to_all x1, waiting for transfers between devices, per_device(): lax.all_to_all(first.reshape(row_count // groups, groups, col_width), 'ro...  17.7 us
    ppermute x4, starting transfers between devices, per_device(): came = lax.ppermute(far, 'x_hi', swap)  14.6 us
    all_to_all x1, starting transfers between devices, per_device(): lax.all_to_all(scale_second.reshape(row_count // groups, groups), 'row',...  11.9 us
    dot_general x4, matrix products, per_device(): jnp.dot(gathered[c], upper_far, preferred_element_type=jnp.float32)  8.08 us
    dot_general x4, matrix products, per_device(): own = jnp.dot(gathered[c], upper_own, preferred_element_type=jnp.float32)  6.74 us
  transfers between devices with their start and end apart: 11, of which 7 were waited for; matrix products, arithmetic and copies ran while one was open for 6% of the time, Pallas kernels for 0%

profile of v1, /device:TPU:10, one launch (start us, length us, event | category | flops | bytes accessed | tf_op | source)
XLA Modules:
  0.0 322.0 jit_solution(11787050918068308856)
XLA Ops:
  0.0 0.8 all_to_all.36
  0.8 0.7 copy.29
  1.5 11.9 %all-to-all-start = ((bf16[64,32,1]{0,2,1:T(2,128)(2,1)}), bf16[64,32,1]{0,2,1:T(2,128)(2,1)S(1)}, u32[]{:S(2)}, u32[]{:S(2)}) async-start(bf16[64,32,1]{0,2,1:T(2,128)(2,1)} %copy.29), calls=%async_computation | async-start | bytes 32768 | tf_op jit(solution)/shard_map/all_to_all | solution.py:40
  13.4 0.7 convert_element_type.109
  14.1 1.4 multiply_convert_fusion
  15.5 1.0 copy.30
  16.5 4.1 %all-to-all-done = bf16[64,32,1]{0,2,1:T(2,128)(2,1)S(1)} async-done(((bf16[64,32,1]{0,2,1:T(2,128)(2,1)}), bf16[64,32,1]{0,2,1:T(2,128)(2,1)S(1)}, u32[]{:S(2)}, u32[]{:S(2)}) %all-to-all-start) | async-done | bytes 4128 | tf_op jit(solution)/shard_map/all_to_all | solution.py:40
  20.5 4.7 %all-to-all-start.1 = ((bf16[64,32,128]{2,0,1:T(8,128)(2,1)}), bf16[64,32,128]{2,0,1:T(8,128)(2,1)S(1)}, u32[]{:S(2)}, u32[]{:S(2)}) async-start(bf16[64,32,128]{2,0,1:T(8,128)(2,1)} %copy.30), calls=%async_computation.1 | async-start | bytes 1048576 | tf_op jit(solution)/shard_map/all_to_all | solution.py:33
  25.3 0.1 bitcast_reduce_fusion
  25.3 0.1 reshape.85
  25.4 17.7 %all-to-all-done.1 = bf16[64,32,128]{2,0,1:T(8,128)(2,1)S(1)} async-done(((bf16[64,32,128]{2,0,1:T(8,128)(2,1)}), bf16[64,32,128]{2,0,1:T(8,128)(2,1)S(1)}, u32[]{:S(2)}, u32[]{:S(2)}) %all-to-all-start.1) | async-done | bytes 524320 | tf_op jit(solution)/shard_map/all_to_all | solution.py:33
  43.1 0.1 fusion.5
  43.2 0.2 copy.32
  43.4 0.2 copy.31
  43.6 0.1 fusion.4
  43.7 0.0 copy-start.1
  43.7 0.8 copy-done.1
  44.5 0.0 copy-start.3
  44.5 0.1 copy.33
  44.7 1.3 broadcast_in_dim.10
  45.9 5.8 %all-to-all-start.2 = ((bf16[64,64,128]{2,1,0:T(8,128)(2,1)}), bf16[64,64,128]{2,1,0:T(8,128)(2,1)S(1)}, u32[]{:S(2)}, u32[]{:S(2)}) async-start(bf16[64,64,128]{2,1,0:T(8,128)(2,1)} %bitcast.8), calls=%async_computation.2 | async-start | bytes 2097152 | tf_op jit(solution)/shard_map/all_to_all | solution.py:63
  51.7 0.0 copy-done.3
  51.7 0.9 fusion.47
  52.6 0.1 copy.38
  52.8 27.8 %all-to-all-done.2 = bf16[64,64,128]{2,1,0:T(8,128)(2,1)S(1)} async-done(((bf16[64,64,128]{2,1,0:T(8,128)(2,1)}), bf16[64,64,128]{2,1,0:T(8,128)(2,1)S(1)}, u32[]{:S(2)}, u32[]{:S(2)}) %all-to-all-start.2) | async-done | bytes 1048608 | tf_op jit(solution)/shard_map/all_to_all | solution.py:63
  80.5 0.0 copy-start
  80.5 1.6 stack.11
  82.1 0.0 copy-done
  82.1 7.5 %all-to-all-start.6 = ((bf16[8,512,256]{1,2,0:T(8,128)(2,1)}), bf16[8,512,256]{1,2,0:T(8,128)(2,1)S(1)}, u32[]{:S(2)}, u32[]{:S(2)}) async-start(bf16[8,512,256]{1,2,0:T(8,128)(2,1)} %stack.11), calls=%async_computation.6 | async-start | bytes 4194304 | tf_op jit(solution)/shard_map/all_to_all | solution.py:26
  89.7 1.1 copy.37
  90.8 47.9 %all-to-all-done.6 = bf16[8,512,256]{1,2,0:T(8,128)(2,1)S(1)} async-done(((bf16[8,512,256]{1,2,0:T(8,128)(2,1)}), bf16[8,512,256]{1,2,0:T(8,128)(2,1)S(1)}, u32[]{:S(2)}, u32[]{:S(2)}) %all-to-all-start.6) | async-done | bytes 2097184 | tf_op jit(solution)/shard_map/all_to_all | solution.py:26
  138.6 1.5 stack.10
  140.1 0.0 copy-start.4
  140.1 5.9 %all-to-all-start.5 = ((bf16[8,512,256]{1,2,0:T(8,128)(2,1)}), bf16[8,512,256]{1,2,0:T(8,128)(2,1)}, u32[]{:S(2)}, u32[]{:S(2)}) async-start(bf16[8,512,256]{1,2,0:T(8,128)(2,1)} %stack.10), calls=%async_computation.5 | async-start | bytes 4194304 | tf_op jit(solution)/shard_map/all_to_all | solution.py:26
  146.0 0.0 copy-done.4
  146.0 0.1 copy.36
  146.2 49.8 %all-to-all-done.5 = bf16[8,512,256]{1,2,0:T(8,128)(2,1)} async-done(((bf16[8,512,256]{1,2,0:T(8,128)(2,1)}), bf16[8,512,256]{1,2,0:T(8,128)(2,1)}, u32[]{:S(2)}, u32[]{:S(2)}) %all-to-all-start.5) | async-done | bytes 2097184 | tf_op jit(solution)/shard_map/all_to_all | solution.py:26
  196.0 1.5 stack.9
  197.6 4.3 %all-to-all-start.4 = ((bf16[8,512,256]{1,2,0:T(8,128)(2,1)}), bf16[8,512,256]{1,2,0:T(8,128)(2,1)}, u32[]{:S(2)}, u32[]{:S(2)}) async-start(bf16[8,512,256]{1,2,0:T(8,128)(2,1)} %stack.9), calls=%async_computation.4 | async-start | bytes 4194304 | tf_op jit(solution)/shard_map/all_to_all | solution.py:26
  201.9 0.1 copy.35
  202.0 48.8 %all-to-all-done.4 = bf16[8,512,256]{1,2,0:T(8,128)(2,1)} async-done(((bf16[8,512,256]{1,2,0:T(8,128)(2,1)}), bf16[8,512,256]{1,2,0:T(8,128)(2,1)}, u32[]{:S(2)}, u32[]{:S(2)}) %all-to-all-start.4) | async-done | bytes 2097184 | tf_op jit(solution)/shard_map/all_to_all | solution.py:26
  250.8 1.5 stack.8
  252.3 5.7 %all-to-all-start.3 = ((bf16[8,512,256]{1,2,0:T(8,128)(2,1)}), bf16[8,512,256]{1,2,0:T(8,128)(2,1)}, u32[]{:S(2)}, u32[]{:S(2)}) async-start(bf16[8,512,256]{1,2,0:T(8,128)(2,1)} %stack.8), calls=%async_computation.3 | async-start | bytes 4194304 | tf_op jit(solution)/shard_map/all_to_all | solution.py:26
  258.0 1.9 copy.34
  259.9 0.5 fusion.3
  260.4 3.6 %collective-permute-start.3 = (bf16[512,128]{0,1:T(8,128)(2,1)S(1)}, bf16[512,128]{0,1:T(8,128)(2,1)S(1)}, u32[]{:S(2)}, u32[]{:S(2)}) collective-permute-start(bf16[512,128]{0,1:T(8,128)(2,1)S(1)} %fusion.3), channel_id=1, source_target_pairs={{0,8},{8,0},{1,9},{9,1},{2,10},{10,2},{3,11},{11,3},{4,12},{12,4},... | collective-permute-start | bytes 393224 | tf_op jit(solution)/shard_map/ppermute | solution.py:75
  264.1 2.7 fusion.2
  266.8 3.7 %collective-permute-start.2 = (bf16[512,128]{0,1:T(8,128)(2,1)}, bf16[512,128]{0,1:T(8,128)(2,1)}, u32[]{:S(2)}, u32[]{:S(2)}) collective-permute-start(bf16[512,128]{0,1:T(8,128)(2,1)} %fusion.2), channel_id=1, source_target_pairs={{0,8},{8,0},{1,9},{9,1},{2,10},{10,2},{3,11},{11,3},{4,12},{12,4},... | collective-permute-start | bytes 393224 | tf_op jit(solution)/shard_map/ppermute | solution.py:75
  270.5 2.7 fusion.1
  273.3 3.6 %collective-permute-start.1 = (bf16[512,128]{0,1:T(8,128)(2,1)}, bf16[512,128]{0,1:T(8,128)(2,1)}, u32[]{:S(2)}, u32[]{:S(2)}) collective-permute-start(bf16[512,128]{0,1:T(8,128)(2,1)} %fusion.1), channel_id=1, source_target_pairs={{0,8},{8,0},{1,9},{9,1},{2,10},{10,2},{3,11},{11,3},{4,12},{12,4},... | collective-permute-start | bytes 393224 | tf_op jit(solution)/shard_map/ppermute | solution.py:75
  276.9 31.5 %all-to-all-done.3 = bf16[8,512,256]{1,2,0:T(8,128)(2,1)} async-done(((bf16[8,512,256]{1,2,0:T(8,128)(2,1)}), bf16[8,512,256]{1,2,0:T(8,128)(2,1)}, u32[]{:S(2)}, u32[]{:S(2)}) %all-to-all-start.3) | async-done | bytes 2097184 | tf_op jit(solution)/shard_map/all_to_all | solution.py:26
  308.4 0.0 copy-start.2
  308.4 2.1 fusion
  310.5 3.6 %collective-permute-start = (bf16[512,128]{0,1:T(8,128)(2,1)S(1)}, bf16[512,128]{0,1:T(8,128)(2,1)S(1)}, u32[]{:S(2)}, u32[]{:S(2)}) collective-permute-start(bf16[512,128]{0,1:T(8,128)(2,1)S(1)} %fusion), channel_id=1, source_target_pairs={{0,8},{8,0},{1,9},{9,1},{2,10},{10,2},{3,11},{11,3},{4,12},{12,4},... | collective-permute-start | bytes 393224 | tf_op jit(solution)/shard_map/ppermute | solution.py:75
  314.1 0.0 collective-permute-done.3
  314.1 0.0 copy-done.2
  314.2 0.5 subtract_convert_fusion
  314.7 0.0 collective-permute-done.2
  314.7 2.1 subtract_convert_fusion.1
  316.8 0.0 collective-permute-done.1
  316.8 2.1 subtract_convert_fusion.2
  318.9 0.0 collective-permute-done
  318.9 2.1 subtract_convert_fusion.3
  321.0 1.0 copy.39
  (3 shorter events, 0.1 us)
Async XLA Ops:
  1.5 19.1 %all-to-all-start = ((bf16[64,32,1]{0,2,1:T(2,128)(2,1)}), bf16[64,32,1]{0,2,1:T(2,128)(2,1)S(1)}, u32[]{:S(2)}, u32[]{:S(2)}) async-start(bf16[64,32,1]{0,2,1:T(2,128)(2,1)} %copy.29), calls=%async_computation | async-start | bytes 32768 | tf_op jit(solution)/shard_map/all_to_all | solution.py:40
  20.5 22.5 %all-to-all-start.1 = ((bf16[64,32,128]{2,0,1:T(8,128)(2,1)}), bf16[64,32,128]{2,0,1:T(8,128)(2,1)S(1)}, u32[]{:S(2)}, u32[]{:S(2)}) async-start(bf16[64,32,128]{2,0,1:T(8,128)(2,1)} %copy.30), calls=%async_computation.1 | async-start | bytes 1048576 | tf_op jit(solution)/shard_map/all_to_all | solution.py:33
  43.7 0.8 copy-start.1
  44.5 7.2 %copy-start.3 = (bf16[2048,256]{1,0:T(8,128)(2,1)S(1)}, bf16[2048,256]{1,0:T(8,128)(2,1)}, u32[]{:S(2)}) copy-start(bf16[2048,256]{1,0:T(8,128)(2,1)} %param.7) | copy-start | bytes 3145732
  45.9 34.6 %all-to-all-start.2 = ((bf16[64,64,128]{2,1,0:T(8,128)(2,1)}), bf16[64,64,128]{2,1,0:T(8,128)(2,1)S(1)}, u32[]{:S(2)}, u32[]{:S(2)}) async-start(bf16[64,64,128]{2,1,0:T(8,128)(2,1)} %bitcast.8), calls=%async_computation.2 | async-start | bytes 2097152 | tf_op jit(solution)/shard_map/all_to_all | solution.py:63
  80.5 1.6 copy-start
  82.1 56.5 %all-to-all-start.6 = ((bf16[8,512,256]{1,2,0:T(8,128)(2,1)}), bf16[8,512,256]{1,2,0:T(8,128)(2,1)S(1)}, u32[]{:S(2)}, u32[]{:S(2)}) async-start(bf16[8,512,256]{1,2,0:T(8,128)(2,1)} %stack.11), calls=%async_computation.6 | async-start | bytes 4194304 | tf_op jit(solution)/shard_map/all_to_all | solution.py:26
  140.1 5.9 %copy-start.4 = (bf16[512,256]{1,0:T(8,128)(2,1)S(1)}, bf16[512,256]{1,0:T(8,128)(2,1)}, u32[]{:S(2)}) copy-start(bf16[512,256]{1,0:T(8,128)(2,1)} %get-tuple-element.6) | copy-start | bytes 786436
  140.1 55.9 %all-to-all-start.5 = ((bf16[8,512,256]{1,2,0:T(8,128)(2,1)}), bf16[8,512,256]{1,2,0:T(8,128)(2,1)}, u32[]{:S(2)}, u32[]{:S(2)}) async-start(bf16[8,512,256]{1,2,0:T(8,128)(2,1)} %stack.10), calls=%async_computation.5 | async-start | bytes 4194304 | tf_op jit(solution)/shard_map/all_to_all | solution.py:26
  197.6 53.2 %all-to-all-start.4 = ((bf16[8,512,256]{1,2,0:T(8,128)(2,1)}), bf16[8,512,256]{1,2,0:T(8,128)(2,1)}, u32[]{:S(2)}, u32[]{:S(2)}) async-start(bf16[8,512,256]{1,2,0:T(8,128)(2,1)} %stack.9), calls=%async_computation.4 | async-start | bytes 4194304 | tf_op jit(solution)/shard_map/all_to_all | solution.py:26
  252.3 56.1 %all-to-all-start.3 = ((bf16[8,512,256]{1,2,0:T(8,128)(2,1)}), bf16[8,512,256]{1,2,0:T(8,128)(2,1)}, u32[]{:S(2)}, u32[]{:S(2)}) async-start(bf16[8,512,256]{1,2,0:T(8,128)(2,1)} %stack.8), calls=%async_computation.3 | async-start | bytes 4194304 | tf_op jit(solution)/shard_map/all_to_all | solution.py:26
  260.4 53.7 %collective-permute-start.3 = (bf16[512,128]{0,1:T(8,128)(2,1)S(1)}, bf16[512,128]{0,1:T(8,128)(2,1)S(1)}, u32[]{:S(2)}, u32[]{:S(2)}) collective-permute-start(bf16[512,128]{0,1:T(8,128)(2,1)S(1)} %fusion.3), channel_id=1, source_target_pairs={{0,8},{8,0},{1,9},{9,1},{2,10},{10,2},{3,11},{11,3},{4,12},{12,4},... | collective-permute-start | bytes 393224 | tf_op jit(solution)/shard_map/ppermute | solution.py:75
  266.8 47.9 %collective-permute-start.2 = (bf16[512,128]{0,1:T(8,128)(2,1)}, bf16[512,128]{0,1:T(8,128)(2,1)}, u32[]{:S(2)}, u32[]{:S(2)}) collective-permute-start(bf16[512,128]{0,1:T(8,128)(2,1)} %fusion.2), channel_id=1, source_target_pairs={{0,8},{8,0},{1,9},{9,1},{2,10},{10,2},{3,11},{11,3},{4,12},{12,4},... | collective-permute-start | bytes 393224 | tf_op jit(solution)/shard_map/ppermute | solution.py:75
  273.3 43.5 %collective-permute-start.1 = (bf16[512,128]{0,1:T(8,128)(2,1)}, bf16[512,128]{0,1:T(8,128)(2,1)}, u32[]{:S(2)}, u32[]{:S(2)}) collective-permute-start(bf16[512,128]{0,1:T(8,128)(2,1)} %fusion.1), channel_id=1, source_target_pairs={{0,8},{8,0},{1,9},{9,1},{2,10},{10,2},{3,11},{11,3},{4,12},{12,4},... | collective-permute-start | bytes 393224 | tf_op jit(solution)/shard_map/ppermute | solution.py:75
  308.4 5.8 %copy-start.2 = (bf16[2048,128]{0,1:T(8,128)(2,1)S(1)}, bf16[2048,128]{0,1:T(8,128)(2,1)}, u32[]{:S(2)}) copy-start(bf16[2048,128]{0,1:T(8,128)(2,1)} %copy-done.1) | copy-start | bytes 1572868
  310.5 8.4 %collective-permute-start = (bf16[512,128]{0,1:T(8,128)(2,1)S(1)}, bf16[512,128]{0,1:T(8,128)(2,1)S(1)}, u32[]{:S(2)}, u32[]{:S(2)}) collective-permute-start(bf16[512,128]{0,1:T(8,128)(2,1)S(1)} %fusion), channel_id=1, source_target_pairs={{0,8},{8,0},{1,9},{9,1},{2,10},{10,2},{3,11},{11,3},{4,12},{12,4},... | collective-permute-start | bytes 393224 | tf_op jit(solution)/shard_map/ppermute | solution.py:75
